TPU v7x, 256 devices: a whole 4x4x8 slice. The times are simulated.
256 devices in a mesh: section: 4 (over z_lo), dp: 64 (over x, y, z_hi, core).
Axes of the slice: x: 4, y: 4, z: 8 (z_hi: 2, z_lo: 4; z = z_hi * 4 + z_lo), core: 2. Of those that a mesh axis runs over, the one named last changes fastest.
Arguments:
- section_inputs: bfloat16 [4, 12544, 2048], P('section', 'dp'), may hold values from -16 to 16
- norm_gain: float32 [4, 2048], P('section'), may hold values from 0.25 to 1.75
- query_gain: float32 [4, 2048], P('section'), may hold values from -5 to 5
- key_gain: float32 [4, 2048], P('section'), may hold values from -5 to 5
- output_weight: bfloat16 [4, 2048, 2048], P('section', 'dp'), may hold values from -0.125 to 0.125
- full_sequence_gradient: bfloat16 [256, 196, 2048], P('dp'), may hold values from -6 to 6
- patch_order: int32 [256, 196], P('dp'), may hold values from 0 to 195, each once within a row
Outputs:
- input_grads: bfloat16 [4, 12544, 2048], P('section', 'dp')
- weight_grads: float32 [4, 2048, 2048], P('section', 'dp')
- gain_grads: float32 [4, 3, 2048], P('section')
Inputs may be any that keep to these rules, and one draw needn't show every extreme that they name: `patch_order`: each row holds every patch number once; the first 49 are the kept patches.
All inputs are finite; a program needn't handle non-finite values.
Results may differ from a plain program's by a relative error of at most 0.0057.
Values may be sent and summed in bfloat16 or wider, within the bound.
A program may use at most 128 MiB of HBM per device.

v0:
```python
import math
import jax
import jax.numpy as jnp
from jax import lax
from jax.sharding import PartitionSpec as P

HEADS = 16
KEPT = 49
PATCHES = 196
MICRO = 2
highest = lax.Precision.HIGHEST


def from_behind(block, axis, distance):
    devices = range(lax.axis_size(axis))
    route = [(i - distance, i) for i in devices if i - distance in devices]
    return lax.ppermute(block, axis, route)


def normalize(inputs):
    values = inputs.astype(jnp.float32)
    centred = values - jnp.mean(values, axis=-1, keepdims=True)
    variance = jnp.mean(centred * centred, axis=-1, keepdims=True)
    inverse = lax.rsqrt(variance + 1e-06)
    return (centred * inverse, inverse)


def attend_forward(normed, gain_row, query_row, key_row, heads):
    row_count, feature_width = normed.shape
    head_width = feature_width // heads
    split_shape = (row_count // KEPT, KEPT, heads, head_width)
    hidden = normed * gain_row
    queries = (hidden * query_row).reshape(split_shape)
    key_rows = (hidden * key_row).reshape(split_shape)
    value_rows = hidden.reshape(split_shape)
    attention_logits = jnp.einsum(
        "bqhd,bkhd->bhqk", queries, key_rows, precision=highest
    ) / math.sqrt(head_width)
    softmaxed = jax.nn.softmax(attention_logits, axis=-1)
    mixed = jnp.einsum("bhqk,bkhd->bqhd", softmaxed, value_rows, precision=highest)
    return (
        hidden,
        queries,
        key_rows,
        value_rows,
        softmaxed,
        mixed.reshape(row_count, feature_width).astype(jnp.bfloat16),
    )


def attend_backward(
    cotangent,
    back,
    normed,
    inverse,
    hidden,
    queries,
    key_rows,
    value_rows,
    softmaxed,
    gain_row,
    query_row,
    key_row,
):
    row_count, feature_width = back.shape
    head_width = queries.shape[-1]
    back_split = back.reshape(queries.shape)
    soft_grad = jnp.einsum("bqhd,bkhd->bhqk", back_split, value_rows, precision=highest)
    value_grad = jnp.einsum("bhqk,bqhd->bkhd", softmaxed, back_split, precision=highest).reshape(
        row_count, feature_width
    )
    score_grad = (
        softmaxed
        * (soft_grad - jnp.sum(soft_grad * softmaxed, axis=-1, keepdims=True))
        / math.sqrt(head_width)
    )
    query_grad = jnp.einsum("bhqk,bkhd->bqhd", score_grad, key_rows, precision=highest).reshape(
        row_count, feature_width
    )
    key_grad = jnp.einsum("bhqk,bqhd->bkhd", score_grad, queries, precision=highest).reshape(
        row_count, feature_width
    )
    hidden_grad = query_grad * query_row + key_grad * key_row + value_grad
    normed_grad = hidden_grad * gain_row
    first_mean = jnp.mean(normed_grad, axis=-1, keepdims=True)
    second_mean = jnp.mean(normed_grad * normed, axis=-1, keepdims=True)
    input_grad = (
        cotangent.astype(jnp.float32) + inverse * (normed_grad - first_mean - normed * second_mean)
    ).astype(jnp.bfloat16)
    sums = jnp.stack(
        [
            jnp.sum(hidden_grad * normed, axis=0),
            jnp.sum(query_grad * hidden, axis=0),
            jnp.sum(key_grad * hidden, axis=0),
        ]
    )
    return (input_grad, sums)


def shards(
    section_inputs,
    norm_gain,
    query_gain,
    key_gain,
    output_weight,
    full_sequence_gradient,
    patch_order,
):
    inputs = section_inputs[0]
    row_count, feature_width = inputs.shape
    image_count = row_count // KEPT
    section = lax.axis_index("section")
    sections = lax.axis_size("section")
    all_images = image_count * lax.axis_size("dp")
    gain_row = norm_gain[0]
    query_row = query_gain[0]
    key_row = key_gain[0]
    weight = lax.all_gather(output_weight[0], "dp", axis=0, tiled=True)
    normed, inverse = normalize(inputs)
    hidden, queries, key_rows, value_rows, softmaxed, mixed = attend_forward(
        normed, gain_row, query_row, key_row, HEADS
    )
    kept = patch_order[:, :KEPT]
    chosen_patches = (
        kept[:, :, None] == jnp.arange(PATCHES, dtype=jnp.int32)[None, None, :]
    ).astype(jnp.bfloat16)
    upper_bound = (
        jnp.einsum(
            "usn,unj->usj",
            chosen_patches,
            full_sequence_gradient,
            preferred_element_type=jnp.float32,
        )
        .astype(jnp.bfloat16)
        .reshape(row_count, feature_width)
    )
    per_unit = image_count // MICRO
    unit_rows = per_unit * KEPT
    unit_count = image_count // per_unit
    step_count = unit_count + sections - 1

    def take_rows(array, unit):
        return lax.dynamic_slice_in_dim(array, unit * unit_rows, unit_rows, 0)

    def take_images(array, unit):
        return lax.dynamic_slice_in_dim(array, unit * per_unit, per_unit, 0)

    def put_rows(array, piece, unit, valid):
        present_value = take_rows(array, unit)
        return lax.dynamic_update_slice_in_dim(
            array, jnp.where(valid, piece, present_value), unit * unit_rows, 0
        )

    def advance(step_index, carry):
        received, cotangents, input_grads, sums, running_weight = carry
        unit = step_index - (sections - 1 - section)
        valid = jnp.logical_and(unit >= 0, unit < unit_count)
        safe_unit = jnp.clip(unit, 0, unit_count - 1)
        cotangent = jnp.where(section == sections - 1, take_rows(upper_bound, safe_unit), received)
        back = lax.dot_general(
            cotangent, weight, (((1,), (1,)), ((), ())), preferred_element_type=jnp.float32
        )
        input_grad, partial_sums = attend_backward(
            cotangent,
            back,
            take_rows(normed, safe_unit),
            take_rows(inverse, safe_unit),
            take_rows(hidden, safe_unit),
            take_images(queries, safe_unit),
            take_images(key_rows, safe_unit),
            take_images(value_rows, safe_unit),
            take_images(softmaxed, safe_unit),
            gain_row,
            query_row,
            key_row,
        )
        cotangents = put_rows(cotangents, cotangent, safe_unit, valid)
        input_grads = put_rows(input_grads, input_grad, safe_unit, valid)
        sums = sums + jnp.where(valid, partial_sums, 0.0)
        received = from_behind(input_grad, "section", -1)
        return (received, cotangents, input_grads, sums, running_weight)

    weight_offset = jnp.zeros((1,), jnp.float32)
    start_carry = (
        jnp.zeros((unit_rows, feature_width), jnp.bfloat16),
        jnp.zeros_like(inputs),
        jnp.zeros_like(inputs),
        jnp.zeros((3, feature_width), jnp.float32),
        weight_offset,
    )
    final_carry = lax.fori_loop(0, step_count, advance, start_carry)
    cotangents = final_carry[1]
    input_grads = final_carry[2]
    gain_total = lax.psum(final_carry[3], "dp") / all_images
    weight_share = (
        lax.psum_scatter(
            lax.dot_general(
                mixed, cotangents, (((0,), (0,)), ((), ())), preferred_element_type=jnp.float32
            ),
            "dp",
            scatter_dimension=0,
            tiled=True,
        )
        / all_images
    )
    return (input_grads[None], weight_share[None], gain_total[None])


def solution(mesh):
    return jax.shard_map(
        shards,
        mesh=mesh,
        in_specs=(
            P("section", "dp", None),
            P("section", None),
            P("section", None),
            P("section", None),
            P("section", "dp", None),
            P("dp", None, None),
            P("dp", None),
        ),
        out_specs=(P("section", "dp", None), P("section", "dp", None), P("section", None, None)),
        check_vma=False,
    )
```

profile of v0, /device:TPU:96, one launch (start us, length us, event | category | flops | bytes accessed | tf_op | source)
XLA Modules:
  0.0 857.8 jit_solution(7415387619002725321)
XLA Ops:
  12.7 4.7 fusion.17
  26.9 4.0 multiply_reduce_fusion.6
  32.1 3.7 fusion.23
  39.3 82.6 %all-gather.3.cloned.1.call-done = bf16[1,2048,2048]{2,1,0:T(8,128)(2,1)} async-done(((bf16[1,32,2048]{2,1,0:T(8,128)(2,1)}), bf16[1,2048,2048]{2,1,0:T(8,128)(2,1)}) %all-gather.3.cloned.1.call-update) | async-done | bytes 8388624 | tf_op jit(solution)/shard_map/all_gather | solution.py:118
  124.6 193.8 %while.22 = (s32[]{:T(128)}, bf16[98,2048]{1,0:T(8,128)(2,1)}, bf16[196,2048]{1,0:T(8,128)(2,1)}, bf16[196,2048]{1,0:T(8,128)(2,1)}, f32[3,2048]{1,0:T(4,128)S(1...) while((s32[]{:T(128)}, bf16[98,2048]{1,0:T(8,128)(2,1)}, ...), condition=%wide.region_11.12_spmd.clone, body=%wide.region_4.11_spmd.clone.sunk | while | flops 1300798208 | bytes 88767504 | solution.py:191
  126.9 6.1 fusion.47
  133.3 3.1 multiply_reduce_fusion.11
  150.6 5.7 collective-permute-start
  156.2 3.3 dynamic_update_slice.22
  159.5 3.3 dynamic_update_slice.23
  167.5 6.1 fusion.47
  173.8 3.1 multiply_reduce_fusion.11
  191.1 5.3 collective-permute-start
  196.4 3.1 dynamic_update_slice.22
  199.6 3.1 dynamic_update_slice.23
  206.9 6.1 fusion.47
  213.2 3.1 multiply_reduce_fusion.11
  230.5 5.3 collective-permute-start
  235.8 3.1 dynamic_update_slice.22
  238.9 3.1 dynamic_update_slice.23
  245.3 6.1 fusion.47
  251.7 3.1 multiply_reduce_fusion.11
  269.0 5.3 collective-permute-start
  274.2 3.1 dynamic_update_slice.22
  277.4 3.1 dynamic_update_slice.23
  283.0 6.1 fusion.47
  306.6 5.3 collective-permute-start
  311.9 3.1 dynamic_update_slice.22
  315.0 3.1 dynamic_update_slice.23
  318.4 9.5 %fusion.30 = f32[2048,2048]{1,0:T(8,128)} fusion(bf16[196,2048]{1,0:T(8,128)(2,1)} %bitcast.137, bf16[196,2048]{1,0:T(8,128)(2,1)} %get-tuple-element.412), kind=kOutput, calls=%fused_computation.62 | convolution fusion | flops 1644167168 | bytes 18382848 | tf_op jit(solution)/shard_map/dot_general | solution.py:197
  328.0 425.0 %psum.7 = f32[3,2048]{1,0:T(4,128)S(1)} all-reduce(f32[3,2048]{1,0:T(4,128)S(1)} %get-tuple-element.413), channel_id=1, replica_groups=mesh['section'=4,'dp'=64] {'dp'}, use_global_device_ids=true, to_apply=%region_13.14 | all-reduce | flops 6144 | bytes 49152 | tf_op jit(solution)/shard_map/psum | solution.py:194
  753.7 95.6 %reduce-scatter.2.cloned.1.call-done = f32[32,2048]{1,0:T(8,128)} async-done(((f32[2048,2048]{1,0:T(8,128)}), f32[32,2048]{1,0:T(8,128)}) %reduce-scatter.2.cloned.1.call-update) | async-done | bytes 262160 | tf_op jit(solution)/shard_map/reduce_scatter | solution.py:196
  (236 shorter events, 115.9 us)
Async XLA Ops:
  7.2 5.5 copy-start
  7.2 114.7 %all-gather.3.cloned.1.call-start = ((), (), s32[]{:S(2)}) async-start(), calls=%async_computation.2 | async-start | bytes 8519680 | tf_op jit(solution)/shard_map/all_gather | solution.py:118
  7.9 841.4 %reduce-scatter.2.cloned.1.call-start = ((), (), s32[]{:S(2)}) async-start(), calls=%async_computation.1 | async-start | bytes 17039360 | tf_op jit(solution)/shard_map/reduce_scatter | solution.py:196
  8.0 2.8 copy-start.8
  8.0 4.7 slice-start
  17.4 2.5 copy-start.11
  21.4 1.8 copy-start.14
  133.2 3.1 copy-start.6
  136.4 1.7 copy-start.5
  146.1 1.9 copy-start.7
  148.7 7.5 copy-start.4
  150.6 14.7 %collective-permute-start = (bf16[98,2048]{1,0:T(8,128)(2,1)}, bf16[98,2048]{1,0:T(8,128)(2,1)}, u32[]{:S(2)}, u32[]{:S(2)}) collective-permute-start(bf16[98,2048]{1,0:T(8,128)(2,1)} %get-tuple-element.688), channel_id=1, source_target_pairs={{64,0},{128,64},{192,128},{65,1},{129,65},{193,129},{66,2},{130,66... | collective-permute-start | bytes 1204232 | tf_op jit(solution)/shard_map/while/body/eval_jaxpr/ppermute | solution.py:17
  173.8 3.1 copy-start.6
  177.0 1.7 copy-start.5
  186.7 1.9 copy-start.7
  189.3 7.2 copy-start.4
  191.1 13.4 %collective-permute-start = (bf16[98,2048]{1,0:T(8,128)(2,1)}, bf16[98,2048]{1,0:T(8,128)(2,1)}, u32[]{:S(2)}, u32[]{:S(2)}) collective-permute-start(bf16[98,2048]{1,0:T(8,128)(2,1)} %get-tuple-element.688), channel_id=1, source_target_pairs={{64,0},{128,64},{192,128},{65,1},{129,65},{193,129},{66,2},{130,66... | collective-permute-start | bytes 1204232 | tf_op jit(solution)/shard_map/while/body/eval_jaxpr/ppermute | solution.py:17
  213.2 3.1 copy-start.6
  226.1 1.9 copy-start.7
  228.6 7.2 copy-start.4
  230.5 12.6 %collective-permute-start = (bf16[98,2048]{1,0:T(8,128)(2,1)}, bf16[98,2048]{1,0:T(8,128)(2,1)}, u32[]{:S(2)}, u32[]{:S(2)}) collective-permute-start(bf16[98,2048]{1,0:T(8,128)(2,1)} %get-tuple-element.688), channel_id=1, source_target_pairs={{64,0},{128,64},{192,128},{65,1},{129,65},{193,129},{66,2},{130,66... | collective-permute-start | bytes 1204232 | tf_op jit(solution)/shard_map/while/body/eval_jaxpr/ppermute | solution.py:17
  251.7 3.1 copy-start.6
  254.8 1.7 copy-start.5
  264.6 1.9 copy-start.7
  267.1 7.2 copy-start.4
  269.0 11.7 %collective-permute-start = (bf16[98,2048]{1,0:T(8,128)(2,1)}, bf16[98,2048]{1,0:T(8,128)(2,1)}, u32[]{:S(2)}, u32[]{:S(2)}) collective-permute-start(bf16[98,2048]{1,0:T(8,128)(2,1)} %get-tuple-element.688), channel_id=1, source_target_pairs={{64,0},{128,64},{192,128},{65,1},{129,65},{193,129},{66,2},{130,66... | collective-permute-start | bytes 1204232 | tf_op jit(solution)/shard_map/while/body/eval_jaxpr/ppermute | solution.py:17
  289.3 3.1 copy-start.6
  292.5 1.7 copy-start.5
  302.2 1.9 copy-start.7
  304.7 7.2 copy-start.4
  306.6 11.6 %collective-permute-start = (bf16[98,2048]{1,0:T(8,128)(2,1)}, bf16[98,2048]{1,0:T(8,128)(2,1)}, u32[]{:S(2)}, u32[]{:S(2)}) collective-permute-start(bf16[98,2048]{1,0:T(8,128)(2,1)} %get-tuple-element.688), channel_id=1, source_target_pairs={{64,0},{128,64},{192,128},{65,1},{129,65},{193,129},{66,2},{130,66... | collective-permute-start | bytes 1204232 | tf_op jit(solution)/shard_map/while/body/eval_jaxpr/ppermute | solution.py:17
  328.0 523.0 %copy-start.1 = (bf16[4,196,2048]{2,0,1:T(4,128)(2,1)S(1)}, bf16[4,196,2048]{2,0,1:T(4,128)(2,1)}, u32[]{:S(2)}) copy-start(bf16[4,196,2048]{2,0,1:T(4,128)(2,1)} %param.14) | copy-start | bytes 9633796
  (19 other events, 25.2 us)
Sparse Core Ops, SparseCore 0:
  11.5 110.3 all-gather.2
  328.1 521.1 reduce-scatter.1
where the time goes:
time: 860 us; the launch traced here: 858 us
  blocking collectives  425 us (49%)
  waiting for transfers between devices  184 us (21%)
  matrix products  95.3 us (11%)
  local copies, waits for them, and re-layouts  80 us (9%)
  other arithmetic  31.3 us (4%)
  starting transfers between devices  26.8 us (3%)
  between operations  14.2 us (2%)
    psum x1, blocking collectives, shards(): gain_total = lax.psum(final_carry[3], 'dp') / all_images  425 us
    reduce_scatter x1, waiting for transfers between devices, shards(): lax.psum_scatter(lax.dot_general(mixed, cotangents, (((0,), (0,)), ((), (...  95.6 us
    all_gather x1, waiting for transfers between devices, shards(): weight = lax.all_gather(output_weight[0], 'dp', axis=0, tiled=True)  82.6 us
    dynamic_update_slice x10, local copies, waits for them, and re-layouts, put_rows(): lax.dynamic_update_slice_in_dim(array, jnp.where(valid, piece, present_va...  31.8 us
    dot_general x5, matrix products, advance(): lax.dot_general(cotangent, weight, (((1,), (1,)), ((), ())), preferred_el...  30.5 us
    ppermute x5, starting transfers between devices, from_behind(): return lax.ppermute(block, axis, route)  26.7 us
    while x110, local copies, waits for them, and re-layouts  22.4 us
    select_n x10, other arithmetic, put_rows(): jnp.where(valid, piece, present_value)  17.9 us
  transfers between devices with their start and end apart: 7, of which 6 were waited for; matrix products, arithmetic and copies ran while one was open for 7% of the time, Pallas kernels for 0%

commit v1 on v0

--- a/solution.py
+++ b/solution.py
@@ -115,7 +115,9 @@
     gain_row = norm_gain[0]
     query_row = query_gain[0]
     key_row = key_gain[0]
-    weight = lax.all_gather(output_weight[0], "dp", axis=0, tiled=True)
+    weight = jnp.concatenate(
+        lax.all_to_all(jnp.stack([output_weight[0]] * lax.axis_size("dp")), "dp", 0, 0), axis=0
+    )
     normed, inverse = normalize(inputs)
     hidden, queries, key_rows, value_rows, softmaxed, mixed = attend_forward(
         normed, gain_row, query_row, key_row, HEADS

time: 860 us -> 952 us (1.11)
  waiting for transfers between devices: 184 us -> 267 us
    all_to_all x0 -> x1, waiting for transfers between devices: none -> 159 us  [shards(): lax.all_to_all(jnp.stack([output_weight[0]] * lax.axis_size('dp')), 'dp',...]
    all_gather x1 -> x0, waiting for transfers between devices: 82.6 us -> none  [shards(): weight = lax.all_gather(output_weight[0], 'dp', axis=0, tiled=True)]
    all_to_all x0 -> x1, starting transfers between devices: none -> 12.1 us  [shards(): lax.all_to_all(jnp.stack([output_weight[0]] * lax.axis_size('dp')), 'dp',...]
    while x110 -> x80, local copies, waits for them, and re-layouts: 22.4 us -> 13.8 us
  transfers between devices with their start and end apart: 7 -> 7, of which waited for: 6 -> 5; matrix products, arithmetic and copies ran while one was open for 7% -> 7% of each run, Pallas kernels for 0% -> 0%
where the time goes in v1:
time: 952 us; the launch traced here: 946 us
  blocking collectives  427 us (45%)
  waiting for transfers between devices  267 us (28%)
  matrix products  96.6 us (10%)
  local copies, waits for them, and re-layouts  71.4 us (8%)
  other arithmetic  38.4 us (4%)
  starting transfers between devices  30.5 us (3%)
  between operations  14.2 us (1%)
    psum x1, blocking collectives, shards(): gain_total = lax.psum(final_carry[3], 'dp') / all_images  427 us
    all_to_all x1, waiting for transfers between devices, shards(): lax.all_to_all(jnp.stack([output_weight[0]] * lax.axis_size('dp')), 'dp',...  159 us
    reduce_scatter x1, waiting for transfers between devices, shards(): lax.psum_scatter(lax.dot_general(mixed, cotangents, (((0,), (0,)), ((), (...  103 us
    dynamic_update_slice x10, local copies, waits for them, and re-layouts, put_rows(): lax.dynamic_update_slice_in_dim(array, jnp.where(valid, piece, present_va...  33.5 us
    dot_general x5, matrix products, advance(): lax.dot_general(cotangent, weight, (((1,), (1,)), ((), ())), preferred_el...  30.5 us
    select_n x10, other arithmetic, put_rows(): jnp.where(valid, piece, present_value)  25 us
  transfers between devices with their start and end apart: 7, of which 5 were waited for; matrix products, arithmetic and copies ran while one was open for 7% of the time, Pallas kernels for 0%

profile of v1, /device:TPU:96, one launch (start us, length us, event | category | flops | bytes accessed | tf_op | source)
XLA Modules:
  0.0 946.3 jit_solution(16603692737164646509)
XLA Ops:
  7.2 5.3 stack.39
  12.5 12.1 %all-to-all-start = ((bf16[64,32,2048]{2,1,0:T(8,128)(2,1)}), bf16[64,32,2048]{2,1,0:T(8,128)(2,1)}, u32[]{:S(2)}, u32[]{:S(2)}) async-start(bf16[64,32,2048]{2,1,0:T(8,128)(2,1)} %stack.39), calls=%async_computation | async-start | bytes 16777216 | tf_op jit(solution)/shard_map/all_to_all | solution.py:119
  38.1 4.7 fusion.17
  45.2 5.4 multiply_reduce_fusion.6
  52.5 3.7 fusion.23
  59.9 158.9 %all-to-all-done = bf16[64,32,2048]{2,1,0:T(8,128)(2,1)} async-done(((bf16[64,32,2048]{2,1,0:T(8,128)(2,1)}), bf16[64,32,2048]{2,1,0:T(8,128)(2,1)}, u32[]{:S(2)}, u32[]{:S(2)}) %all-to-all-start) | async-done | bytes 8388640 | tf_op jit(solution)/shard_map/all_to_all | solution.py:119
  220.8 176.3 %while.22 = (s32[]{:T(128)}, bf16[98,2048]{1,0:T(8,128)(2,1)S(1)}, bf16[196,2048]{1,0:T(8,128)(2,1)}, bf16[196,2048]{1,0:T(8,128)(2,1)}, f32[3,2048]{1,0:T(4,128...) while((s32[]{:T(128)}, bf16[98,2048]{1,0:T(8,128)(2,1)S(1)}, ...), condition=%wide.region_11.12_spmd.clone, body=%wide.region_4.11_spmd.clone.sunk | while | flops 1300798208 | bytes 80739248 | solution.py:193
  223.1 6.1 fusion.47
  229.4 3.1 multiply_reduce_fusion.11
  246.1 3.4 dynamic_update_slice.23
  249.5 3.4 dynamic_update_slice.22
  257.4 6.1 fusion.47
  263.8 3.1 multiply_reduce_fusion.11
  279.0 4.3 collective-permute-start
  283.4 3.3 dynamic_update_slice.23
  286.7 3.3 dynamic_update_slice.22
  293.9 6.1 fusion.47
  300.2 3.1 multiply_reduce_fusion.11
  315.5 4.3 collective-permute-start
  319.8 3.3 dynamic_update_slice.23
  323.2 3.3 dynamic_update_slice.22
  329.5 6.1 fusion.47
  351.1 4.3 collective-permute-start
  355.4 3.3 dynamic_update_slice.23
  358.8 3.3 dynamic_update_slice.22
  364.4 6.1 fusion.47
  386.0 4.1 collective-permute-start
  390.1 3.3 dynamic_update_slice.23
  393.5 3.3 dynamic_update_slice.22
  397.1 9.5 %fusion.30 = f32[2048,2048]{1,0:T(8,128)} fusion(bf16[196,2048]{1,0:T(8,128)(2,1)} %bitcast.137, bf16[196,2048]{1,0:T(8,128)(2,1)} %get-tuple-element.412), kind=kOutput, calls=%fused_computation.62 | convolution fusion | flops 1644167168 | bytes 18382848 | tf_op jit(solution)/shard_map/dot_general | solution.py:199
  406.6 427.5 %psum.7 = f32[3,2048]{1,0:T(4,128)S(1)} all-reduce(f32[3,2048]{1,0:T(4,128)S(1)} %get-tuple-element.413), channel_id=1, replica_groups=mesh['section'=4,'dp'=64] {'dp'}, use_global_device_ids=true, to_apply=%region_13.14 | all-reduce | flops 6144 | bytes 49152 | tf_op jit(solution)/shard_map/psum | solution.py:196
  834.8 103.1 %reduce-scatter.2.cloned.1.call-done = f32[32,2048]{1,0:T(8,128)} async-done(((f32[2048,2048]{1,0:T(8,128)}), f32[32,2048]{1,0:T(8,128)}) %reduce-scatter.2.cloned.1.call-update) | async-done | bytes 262160 | tf_op jit(solution)/shard_map/reduce_scatter | solution.py:198
  (214 shorter events, 110.3 us)
Async XLA Ops:
  7.2 30.9 %copy-start = (bf16[4,196,2048]{2,0,1:T(4,128)(2,1)S(1)}, bf16[4,196,2048]{2,0,1:T(4,128)(2,1)}, u32[]{:S(2)}) copy-start(bf16[4,196,2048]{2,0,1:T(4,128)(2,1)} %param.14) | copy-start | bytes 9633796
  12.5 206.3 %all-to-all-start = ((bf16[64,32,2048]{2,1,0:T(8,128)(2,1)}), bf16[64,32,2048]{2,1,0:T(8,128)(2,1)}, u32[]{:S(2)}, u32[]{:S(2)}) async-start(bf16[64,32,2048]{2,1,0:T(8,128)(2,1)} %stack.39), calls=%async_computation | async-start | bytes 16777216 | tf_op jit(solution)/shard_map/all_to_all | solution.py:119
  24.6 913.2 %reduce-scatter.2.cloned.1.call-start = ((), (), s32[]{:S(2)}) async-start(), calls=%async_computation.2 | async-start | bytes 17039360 | tf_op jit(solution)/shard_map/reduce_scatter | solution.py:198
  24.7 2.6 copy-start.11
  32.2 2.3 copy-start.3
  32.2 4.1 copy-start.8
  32.2 2.2 copy-start.15
  34.5 3.5 copy-start.10
  36.3 1.8 slice-start
  42.7 2.4 copy-start.9
  229.4 3.1 copy-start.6
  232.6 1.7 copy-start.5
  239.2 1.4 copy-start.2
  239.2 1.9 copy-start.7
  244.7 10.5 %collective-permute-start = (bf16[98,2048]{1,0:T(8,128)(2,1)}, bf16[98,2048]{1,0:T(8,128)(2,1)S(1)}, u32[]{:S(2)}, u32[]{:S(2)}) collective-permute-start(bf16[98,2048]{1,0:T(8,128)(2,1)} %get-tuple-element.688), channel_id=1, source_target_pairs={{64,0},{128,64},{192,128},{65,1},{129,65},{193,129},{66,2},{130,66... | collective-permute-start | bytes 1204232 | tf_op jit(solution)/shard_map/while/body/eval_jaxpr/ppermute | solution.py:17
  263.7 3.1 copy-start.6
  266.9 1.7 copy-start.5
  273.5 1.9 copy-start.7
  279.0 12.6 %collective-permute-start = (bf16[98,2048]{1,0:T(8,128)(2,1)}, bf16[98,2048]{1,0:T(8,128)(2,1)S(1)}, u32[]{:S(2)}, u32[]{:S(2)}) collective-permute-start(bf16[98,2048]{1,0:T(8,128)(2,1)} %get-tuple-element.688), channel_id=1, source_target_pairs={{64,0},{128,64},{192,128},{65,1},{129,65},{193,129},{66,2},{130,66... | collective-permute-start | bytes 1204232 | tf_op jit(solution)/shard_map/while/body/eval_jaxpr/ppermute | solution.py:17
  300.2 3.1 copy-start.6
  303.4 1.7 copy-start.5
  310.0 1.9 copy-start.7
  315.5 11.7 %collective-permute-start = (bf16[98,2048]{1,0:T(8,128)(2,1)}, bf16[98,2048]{1,0:T(8,128)(2,1)S(1)}, u32[]{:S(2)}, u32[]{:S(2)}) collective-permute-start(bf16[98,2048]{1,0:T(8,128)(2,1)} %get-tuple-element.688), channel_id=1, source_target_pairs={{64,0},{128,64},{192,128},{65,1},{129,65},{193,129},{66,2},{130,66... | collective-permute-start | bytes 1204232 | tf_op jit(solution)/shard_map/while/body/eval_jaxpr/ppermute | solution.py:17
  335.8 3.1 copy-start.6
  339.0 1.7 copy-start.5
  345.6 1.9 copy-start.7
  351.1 11.0 %collective-permute-start = (bf16[98,2048]{1,0:T(8,128)(2,1)}, bf16[98,2048]{1,0:T(8,128)(2,1)S(1)}, u32[]{:S(2)}, u32[]{:S(2)}) collective-permute-start(bf16[98,2048]{1,0:T(8,128)(2,1)} %get-tuple-element.688), channel_id=1, source_target_pairs={{64,0},{128,64},{192,128},{65,1},{129,65},{193,129},{66,2},{130,66... | collective-permute-start | bytes 1204232 | tf_op jit(solution)/shard_map/while/body/eval_jaxpr/ppermute | solution.py:17
  370.7 3.1 copy-start.6
  373.9 1.7 copy-start.5
  380.5 1.9 copy-start.7
  386.0 10.8 %collective-permute-start = (bf16[98,2048]{1,0:T(8,128)(2,1)}, bf16[98,2048]{1,0:T(8,128)(2,1)S(1)}, u32[]{:S(2)}, u32[]{:S(2)}) collective-permute-start(bf16[98,2048]{1,0:T(8,128)(2,1)} %get-tuple-element.688), channel_id=1, source_target_pairs={{64,0},{128,64},{192,128},{65,1},{129,65},{193,129},{66,2},{130,66... | collective-permute-start | bytes 1204232 | tf_op jit(solution)/shard_map/while/body/eval_jaxpr/ppermute | solution.py:17
  406.6 532.9 %copy-start.1 = (bf16[4,196,2048]{2,0,1:T(4,128)(2,1)S(1)}, bf16[4,196,2048]{2,0,1:T(4,128)(2,1)}, u32[]{:S(2)}) copy-start(bf16[4,196,2048]{2,0,1:T(4,128)(2,1)} %param.14) | copy-start | bytes 9633796
  (8 other events, 9.9 us)
Sparse Core Ops, SparseCore 0:
  406.8 531.0 reduce-scatter.1
